TPU v7x, 32 devices: a whole 2x2x4 slice. The times are simulated.
32 devices in a mesh: dp: 4 (over y, x), filter: 8 (over z, core).
Axes of the slice: x: 2, y: 2, z: 4, core: 2. Of those that a mesh axis runs over, the one named last changes fastest.
Arguments:
- fields: bfloat16 [4, 32, 32, 1024], P('dp', None, None, 'filter'), may hold values from -6 to 6
- weight_one: bfloat16 [3, 3, 1024, 1024], P(None, None, 'dp', 'filter'), may hold values from -0.0625 to 0.0625
- weight_two: bfloat16 [3, 3, 1024, 1024], P(None, None, 'dp', 'filter'), may hold values from -0.0625 to 0.0625
- cotangent: bfloat16 [4, 32, 32, 1024], P('dp', None, None, 'filter'), may hold values from -6 to 6
Outputs:
- output: bfloat16 [4, 32, 32, 1024], P('dp', None, None, 'filter')
- grad_one: float32 [3, 3, 1024, 1024], P(None, None, 'dp', 'filter')
- grad_two: float32 [3, 3, 1024, 1024], P(None, None, 'dp', 'filter')
All inputs are finite; a program needn't handle non-finite values.
Results may differ from a plain program's by a relative error of at most 0.018.
Values may be sent and summed in bfloat16 or wider, within the bound.
No kernel may reach another device: no remote copies, remote signals or barrier semaphores. Data moves between devices by JAX's collectives and lax.ppermute only.
A program may use at most 128 MiB of HBM per device.

v0:
```python
import jax
import jax.numpy as jnp
from jax import lax
from jax.sharding import PartitionSpec as P


def shift_cells(values, row_step, col_step):
    size = values.shape[1]
    padded = jnp.pad(values, ((0, 0), (1, 1), (1, 1), (0, 0)))
    return padded[:, 1 + row_step : 1 + row_step + size, 1 + col_step : 1 + col_step + size, :]


def conv_taps(inputs, weights):
    products = jnp.einsum("bhwc,pqcd->bhwpqd", inputs, weights, preferred_element_type=jnp.float32)
    result = jnp.zeros(inputs.shape[:3] + (weights.shape[3],), jnp.float32)
    for row_tap in range(3):
        for col_tap in range(3):
            result = result + shift_cells(
                products[:, :, :, row_tap, col_tap, :], row_tap - 1, col_tap - 1
            )
    return result


def shifted_stack(grads):
    pieces = []
    for row_tap in range(3):
        for col_tap in range(3):
            pieces.append(shift_cells(grads, 1 - row_tap, 1 - col_tap))
    return jnp.stack(pieces, axis=3).reshape(grads.shape[:3] + (3, 3, grads.shape[3]))


def transposed(grads, weights):
    stacked = shifted_stack(grads)
    return jnp.einsum("bhwpqd,pqcd->bhwc", stacked, weights, preferred_element_type=jnp.float32)


def filter_grads(inputs, grads):
    stacked = shifted_stack(grads)
    return jnp.einsum("bhwc,bhwpqd->pqcd", inputs, stacked, preferred_element_type=jnp.float32)


def body(fields, weight_one, weight_two, cotangent):
    full_one = lax.all_gather(weight_one, "dp", axis=2, tiled=True)
    gathered = lax.all_gather(fields, "filter", axis=3, tiled=True)
    pre_one = conv_taps(gathered, full_one)
    hidden = jax.nn.silu(pre_one).astype(jnp.bfloat16)
    hidden_all = lax.all_gather(hidden, "filter", axis=3, tiled=True)
    full_two = lax.all_gather(weight_two, "dp", axis=2, tiled=True)
    output = conv_taps(hidden_all, full_two).astype(jnp.bfloat16)
    grad_two = lax.psum_scatter(
        filter_grads(hidden_all, cotangent).astype(jnp.bfloat16),
        "dp",
        scatter_dimension=2,
        tiled=True,
    ).astype(jnp.float32)
    partial_back = transposed(cotangent, full_two)
    back = lax.psum_scatter(
        partial_back.astype(jnp.bfloat16), "filter", scatter_dimension=3, tiled=True
    ).astype(jnp.float32)
    sigma = jax.nn.sigmoid(pre_one)
    back_pre = (back * sigma * (1.0 + pre_one * (1.0 - sigma))).astype(jnp.bfloat16)
    grad_one = lax.psum_scatter(
        filter_grads(gathered, back_pre).astype(jnp.bfloat16), "dp", scatter_dimension=2, tiled=True
    ).astype(jnp.float32)
    return (output, grad_one, grad_two)


def solution(mesh):
    placed = (
        P("dp", None, None, "filter"),
        P(None, None, "dp", "filter"),
        P(None, None, "dp", "filter"),
        P("dp", None, None, "filter"),
    )
    return jax.shard_map(
        body,
        mesh=mesh,
        in_specs=placed,
        out_specs=(
            P("dp", None, None, "filter"),
            P(None, None, "dp", "filter"),
            P(None, None, "dp", "filter"),
        ),
        check_vma=False,
    )
```

profile of v0, /device:TPU:0, one launch (start us, length us, event | category | flops | bytes accessed | tf_op | source)
XLA Modules:
  0.0 284.4 jit_solution(1730159838617975054)
XLA Ops:
  7.2 0.7 all-gather.11.cloned.1.call-update
  8.0 0.7 all-gather.7.cloned.1.call-update
  8.7 0.7 all-gather.5.cloned.1.call-update
  9.4 1.0 fusion.41
  10.5 1.0 fusion.43
  12.1 38.0 %all-gather.11.cloned.1.call-done = bf16[3,3,1024,128]{3,2,1,0:T(8,128)(2,1)} async-done(((bf16[3,3,256,128]{3,2,1,0:T(8,128)(2,1)}), bf16[3,3,1024,128]{3,2,1,0:T(8,128)(2,1)}) %all-gather.11.cloned.1.call-update) | async-done | bytes 2359312 | tf_op jit(solution)/shard_map/all_gather | solution.py:48
  50.1 5.3 %fusion.16 = bf16[1,32,32,1024]{3,2,1,0:T(8,128)(2,1)S(1)} fusion(bf16[32,32,3,3,128]{4,1,0,3,2:T(8,128)(2,1)} %bitcast.223, bf16[3,3,1024,128]{3,2,1,0:T(8,128)(2,1)} %all-gather.11.cloned.1.call-done), kind=kOutput, calls=%fused_computation.15 | convolution fusion | flops 2416967680 | bytes 6815744 | tf_op jit(solution)/shard_map/bhwpqd,pqcd->bhwc/dot_general | solution.py:34
  55.4 12.2 %copy.60 = bf16[1,32,32,1024]{2,1,0,3:T(8,128)(2,1)} copy(bf16[1,32,32,1024]{3,2,1,0:T(8,128)(2,1)S(1)} %fusion.16) | data formatting | bytes 4194304
  67.5 12.5 %reshape.42 = bf16[1024,1024]{1,0:T(8,128)(2,1)} reshape(bf16[1024,1,32,32]{3,2,1,0:T(8,128)(2,1)} %bitcast.220) | data formatting | bytes 4194304
  80.0 9.4 %all-gather.7.cloned.1.call-done = bf16[3,3,1024,128]{3,2,1,0:T(8,128)(2,1)} async-done(((bf16[3,3,256,128]{3,2,1,0:T(8,128)(2,1)}), bf16[3,3,1024,128]{3,2,1,0:T(8,128)(2,1)}) %all-gather.7.cloned.1.call-update) | async-done | bytes 2359312 | tf_op jit(solution)/shard_map/all_gather | solution.py:43
  89.4 32.5 %all-gather.5.cloned.1.call-done = bf16[1,32,32,1024]{3,2,1,0:T(8,128)(2,1)} async-done(((bf16[1,32,32,128]{3,2,1,0:T(8,128)(2,1)}), bf16[1,32,32,1024]{3,2,1,0:T(8,128)(2,1)}) %all-gather.5.cloned.1.call-update) | async-done | bytes 2097168 | tf_op jit(solution)/shard_map/all_gather | solution.py:44
  121.9 5.2 %fusion.10 = f32[1,32,32,3,3,128]{5,2,4,3,1,0:T(8,128)S(1)} fusion(bf16[3,3,1024,128]{3,2,1,0:T(8,128)(2,1)} %all-gather.7.cloned.1.call-done, bf16[1,32,32,1024]{3,2,1,0:T(8,128)(2,1)} %all-gather.5.cloned.1.call-done), kind=kOutput, calls=%fused_computation.13 | convolution fusion | flops 2415919104 | bytes 9175040 | tf_op jit(solution)/shard_map/bhwc,pqcd->bhwpqd/dot_general | solution.py:14
  127.1 2.1 copy-done.1
  129.2 1.8 slice_bitcast_fusion.17
  130.9 28.0 %reduce-scatter.10.cloned.1.call-done = bf16[128,1024]{1,0:T(8,128)(2,1)} async-done(((bf16[1024,1024]{1,0:T(8,128)(2,1)}), bf16[128,1024]{1,0:T(8,128)(2,1)}) %reduce-scatter.10.cloned.1.call-update) | async-done | bytes 262160
  158.9 1.8 reshape.43
  160.7 1.8 copy.61
  162.5 2.3 multiply_convert_fusion
  164.8 0.8 multiply_convert_fusion.1
  166.6 0.9 copy-done.5
  167.5 4.0 %fusion = bf16[3,3,1024,128]{2,3,1,0:T(8,128)(2,1)} fusion(bf16[32,32,3,3,128]{4,1,0,3,2:T(8,128)(2,1)S(1)} %bitcast.225, bf16[1,32,32,1024]{3,2,1,0:T(8,128)(2,1)S(1)} %copy-done.5), kind=kOutput, calls=%fused_computation.3 | convolution fusion | flops 2417098752 | bytes 6815744 | tf_op jit(solution)/shard_map/bhwc,bhwpqd->pqcd/dot_general | solution.py:39
  171.6 23.8 %all-gather.9.cloned.1.call-done = bf16[1,32,32,1024]{3,2,1,0:T(8,128)(2,1)} async-done(((bf16[1,32,32,128]{3,2,1,0:T(8,128)(2,1)}), bf16[1,32,32,1024]{3,2,1,0:T(8,128)(2,1)}) %all-gather.9.cloned.1.call-update) | async-done | bytes 2097168 | tf_op jit(solution)/shard_map/all_gather | solution.py:47
  195.4 4.2 %fusion.4 = bf16[3,3,128,1024,1]{3,2,0,1,4:T(8,128)(2,1)S(1)} fusion(bf16[32,32,3,3,128]{4,1,0,3,2:T(8,128)(2,1)S(1)} %bitcast.224, bf16[1,32,32,1024]{3,2,1,0:T(8,128)(2,1)} %all-gather.9.cloned.1.call-done), kind=kOutput, calls=%fused_computation.7 | convolution fusion | flops 2415919104 | bytes 6815744 | tf_op jit(solution)/shard_map/bhwc,bhwpqd->pqcd/dot_general | solution.py:39
  199.6 1.7 copy.83
  201.4 1.6 copy-done.4
  203.0 4.8 %fusion.13 = f32[1,32,32,3,3,128]{5,2,4,3,1,0:T(8,128)S(1)} fusion(bf16[3,3,1024,128]{3,2,1,0:T(8,128)(2,1)S(1)} %copy-done.4, bf16[1,32,32,1024]{3,2,1,0:T(8,128)(2,1)} %all-gather.9.cloned.1.call-done), kind=kOutput, calls=%fused_computation.14 | convolution fusion | flops 2415919104 | bytes 9175040 | tf_op jit(solution)/shard_map/bhwc,pqcd->bhwpqd/dot_general | solution.py:14
  207.8 0.7 slice_bitcast_fusion
  208.5 1.3 fusion.39
  209.8 25.0 %reduce-scatter.6.cloned.1.call-done = bf16[3,3,256,128]{2,3,1,0:T(8,128)(2,1)} async-done(((bf16[3,3,1024,128]{2,3,1,0:T(8,128)(2,1)}), bf16[3,3,256,128]{2,3,1,0:T(8,128)(2,1)}) %reduce-scatter.6.cloned.1.call-update) | async-done | bytes 589840 | tf_op jit(solution)/shard_map/reduce_scatter | solution.py:62
  234.8 2.3 copy.45
  237.1 38.2 %reduce-scatter.8.cloned.1.call-done = bf16[3,3,256,128]{2,3,1,0:T(8,128)(2,1)} async-done(((bf16[3,3,1024,128]{2,3,1,0:T(8,128)(2,1)}), bf16[3,3,256,128]{2,3,1,0:T(8,128)(2,1)}) %reduce-scatter.8.cloned.1.call-update) | async-done | bytes 589840 | tf_op jit(solution)/shard_map/reduce_scatter | solution.py:50
  275.3 2.3 copy.46
  (36 shorter events, 1.8 us)
Async XLA Ops:
  7.2 4.3 %copy-start = (bf16[1,32,32,128]{3,2,1,0:T(8,128)(2,1)S(1)}, bf16[1,32,32,128]{3,2,1,0:T(8,128)(2,1)}, u32[]{:S(2)}) copy-start(bf16[1,32,32,128]{3,2,1,0:T(8,128)(2,1)} %param.7) | copy-start | bytes 786436
  7.2 42.9 %all-gather.11.cloned.1.call-start = ((), (), s32[]{:S(2)}) async-start(), calls=%async_computation.6 | async-start | bytes 2949120 | tf_op jit(solution)/shard_map/all_gather | solution.py:48
  7.9 81.5 %all-gather.7.cloned.1.call-start = ((), (), s32[]{:S(2)}) async-start(), calls=%async_computation.4 | async-start | bytes 2949120 | tf_op jit(solution)/shard_map/all_gather | solution.py:43
  8.7 113.2 %all-gather.5.cloned.1.call-start = ((), (), s32[]{:S(2)}) async-start(), calls=%async_computation.3 | async-start | bytes 2359296 | tf_op jit(solution)/shard_map/all_gather | solution.py:44
  9.4 149.5 %reduce-scatter.10.cloned.1.call-start = ((), (), s32[]{:S(2)}) async-start(), calls=%async_computation.9 | async-start | bytes 2359296
  12.1 38.0 %copy-start.2 = (bf16[1,32,32,9,128]{4,2,1,3,0:T(8,128)(2,1)}, bf16[1,32,32,9,128]{4,2,1,3,0:T(8,128)(2,1)S(1)}, u32[]{:S(2)}) copy-start(bf16[1,32,32,9,128]{4,2,1,3,0:T(8,128)(2,1)S(1)} %fusion.55) | copy-start | bytes 7077892
  80.0 115.4 %all-gather.9.cloned.1.call-start = ((), (), s32[]{:S(2)}) async-start(), calls=%async_computation.5 | async-start | bytes 2359296 | tf_op jit(solution)/shard_map/all_gather | solution.py:47
  127.1 2.1 copy-start.1
  165.7 69.1 %reduce-scatter.6.cloned.1.call-start = ((), (), s32[]{:S(2)}) async-start(), calls=%async_computation.7 | async-start | bytes 2949120 | tf_op jit(solution)/shard_map/reduce_scatter | solution.py:62
  165.9 1.6 copy-start.5
  171.5 23.9 %copy-start.3 = (bf16[1,32,32,9,128]{4,2,1,3,0:T(8,128)(2,1)S(1)}, bf16[1,32,32,9,128]{4,2,1,3,0:T(8,128)(2,1)}, u32[]{:S(2)}) copy-start(bf16[1,32,32,9,128]{4,2,1,3,0:T(8,128)(2,1)} %copy-done.2) | copy-start | bytes 7077892
  171.5 103.8 %reduce-scatter.8.cloned.1.call-start = ((), (), s32[]{:S(2)}) async-start(), calls=%async_computation.8 | async-start | bytes 2949120 | tf_op jit(solution)/shard_map/reduce_scatter | solution.py:50
  201.3 1.7 copy-start.4
Sparse Core Ops, SparseCore 0:
  9.9 40.1 all-gather.10
  51.9 37.4 all-gather.6
  91.0 30.8 all-gather.4
  124.0 34.8 reduce-scatter.9
  165.8 29.5 all-gather.8
  198.3 36.4 reduce-scatter.5
  237.9 37.3 reduce-scatter.7
where the time goes:
time: 285 us; the launch traced here: 284 us
  waiting for transfers between devices  197 us (69%)
  local copies, waits for them, and re-layouts  44.9 us (16%)
  matrix products  23.5 us (8%)
  between operations  14.3 us (5%)
  other arithmetic  4.4 us (2%)
    unnamed x34, local copies, waits for them, and re-layouts  40.6 us
    reduce_scatter x1, waiting for transfers between devices, body(): lax.psum_scatter(filter_grads(hidden_all, cotangent).astype(jnp.bfloat16)...  38.2 us
    all_gather x1, waiting for transfers between devices, body(): full_two = lax.all_gather(weight_two, 'dp', axis=2, tiled=True)  38 us
    all_gather x1, waiting for transfers between devices, body(): gathered = lax.all_gather(fields, 'filter', axis=3, tiled=True)  32.5 us
    unnamed x8, waiting for transfers between devices  30.1 us
    reduce_scatter x1, waiting for transfers between devices, body(): lax.psum_scatter(filter_grads(gathered, back_pre).astype(jnp.bfloat16), '...  25 us
    all_gather x1, waiting for transfers between devices, body(): hidden_all = lax.all_gather(hidden, 'filter', axis=3, tiled=True)  23.8 us
    dot_general x2, matrix products, conv_taps(): jnp.einsum('bhwc,pqcd->bhwpqd', inputs, weights, preferred_element_type=j...  9.99 us
  transfers between devices with their start and end apart: 7, of which 7 were waited for; matrix products, arithmetic and copies ran while one was open for 21% of the time, Pallas kernels for 0%

commit v1 on v0

--- a/solution.py
+++ b/solution.py
@@ -45,7 +45,12 @@
     pre_one = conv_taps(gathered, full_one)
     hidden = jax.nn.silu(pre_one).astype(jnp.bfloat16)
     hidden_all = lax.all_gather(hidden, "filter", axis=3, tiled=True)
-    full_two = lax.all_gather(weight_two, "dp", axis=2, tiled=True)
+    ring = [weight_two]
+    for hop in range(3):
+        ring.append(lax.ppermute(ring[-1], "dp", [(dev, (dev + 1) % 4) for dev in range(4)]))
+    full_two = jnp.roll(
+        jnp.concatenate(ring[::-1], axis=2), (lax.axis_index("dp") + 1) * ring[0].shape[2], axis=2
+    )
     output = conv_taps(hidden_all, full_two).astype(jnp.bfloat16)
     grad_two = lax.psum_scatter(
         filter_grads(hidden_all, cotangent).astype(jnp.bfloat16),

time: 285 us -> 265 us (0.930)
  waiting for transfers between devices: 197 us -> 160 us
  local copies, waits for them, and re-layouts: 44.9 us -> 54.6 us
  starting transfers between devices: 0.46 us -> 8.27 us
    ppermute x0 -> x3, waiting for transfers between devices: none -> 44.2 us  [body(): lax.ppermute(ring[-1], 'dp', [(dev, (dev + 1) % 4) for dev in range(4)])]
    all_gather x1 -> x0, waiting for transfers between devices: 38 us -> none  [body(): full_two = lax.all_gather(weight_two, 'dp', axis=2, tiled=True)]
    all_gather x1, waiting for transfers between devices: 32.5 us -> 0.02 us  [body(): gathered = lax.all_gather(fields, 'filter', axis=3, tiled=True)]
    all_gather x1, waiting for transfers between devices: 9.39 us -> 0.02 us  [body(): full_one = lax.all_gather(weight_one, 'dp', axis=2, tiled=True)]
    unnamed x34 -> x41, local copies, waits for them, and re-layouts: 40.6 us -> 49.5 us
    ppermute x0 -> x3, starting transfers between devices: none -> 7.85 us  [body(): lax.ppermute(ring[-1], 'dp', [(dev, (dev + 1) % 4) for dev in range(4)])]
    unnamed x8 -> x7, waiting for transfers between devices: 30.1 us -> 28.8 us
  transfers between devices with their start and end apart: 7 -> 9, of which waited for: 7 -> 7; matrix products, arithmetic and copies ran while one was open for 21% -> 25% of each run, Pallas kernels for 0% -> 0%
where the time goes in v1:
time: 265 us
  waiting for transfers between devices  160 us (60%)
  local copies, waits for them, and re-layouts  54.6 us (21%)
  matrix products  23.5 us (9%)
  between operations  14.3 us (5%)
  starting transfers between devices  8.27 us (3%)
  other arithmetic  4.4 us (2%)
    unnamed x41, local copies, waits for them, and re-layouts  49.5 us
    ppermute x3, waiting for transfers between devices, body(): lax.ppermute(ring[-1], 'dp', [(dev, (dev + 1) % 4) for dev in range(4)])  44.2 us
    reduce_scatter x1, waiting for transfers between devices, body(): lax.psum_scatter(filter_grads(hidden_all, cotangent).astype(jnp.bfloat16)...  38 us
    unnamed x7, waiting for transfers between devices  28.8 us
    reduce_scatter x1, waiting for transfers between devices, body(): lax.psum_scatter(filter_grads(gathered, back_pre).astype(jnp.bfloat16), '...  24.6 us
    all_gather x1, waiting for transfers between devices, body(): hidden_all = lax.all_gather(hidden, 'filter', axis=3, tiled=True)  23.9 us
    dot_general x2, matrix products, conv_taps(): jnp.einsum('bhwc,pqcd->bhwpqd', inputs, weights, preferred_element_type=j...  9.76 us
    dot_general x2, matrix products, filter_grads(): jnp.einsum('bhwc,bhwpqd->pqcd', inputs, stacked, preferred_element_type=j...  8.92 us
  transfers between devices with their start and end apart: 9, of which 7 were waited for; matrix products, arithmetic and copies ran while one was open for 25% of the time, Pallas kernels for 0%

profile of v1, /device:TPU:0, one launch (start us, length us, event | category | flops | bytes accessed | tf_op | source)
XLA Modules:
  0.0 264.6 jit_solution(16128029211350233633)
XLA Ops:
  8.7 3.0 %collective-permute-start = (bf16[3,3,256,128]{3,2,1,0:T(8,128)(2,1)}, bf16[3,3,256,128]{3,2,1,0:T(8,128)(2,1)S(1)}, u32[]{:S(2)}, u32[]{:S(2)}) collective-permute-start(bf16[3,3,256,128]{3,2,1,0:T(8,128)(2,1)} %param.6), channel_id=1, source_target_pairs={{0,8},{8,16},{16,24},{24,0},{1,9},{9,17},{17,25},{25,1},{2,10},{10... | collective-permute-start | bytes 1769480 | tf_op jit(solution)/shard_map/ppermute | solution.py:50
  11.7 18.0 %collective-permute-done = bf16[3,3,256,128]{3,2,1,0:T(8,128)(2,1)S(1)} collective-permute-done((bf16[3,3,256,128]{3,2,1,0:T(8,128)(2,1)}, bf16[3,3,256,128]{3,2,1,0:T(8,128)(2,1)S(1)}, u32[]{:S(2)}, u32[]{:S(2)}) %collective-permute-start) | collective-permute-done | bytes 589856 | tf_op jit(solution)/shard_map/ppermute | solution.py:50
  29.7 2.4 collective-permute-start.1
  32.1 1.7 fusion.43
  33.8 1.6 fusion.45
  35.4 1.7 fusion.47
  37.9 13.2 %collective-permute-done.1 = bf16[3,3,256,128]{3,2,1,0:T(8,128)(2,1)S(1)} collective-permute-done((bf16[3,3,256,128]{3,2,1,0:T(8,128)(2,1)S(1)}, bf16[3,3,256,128]{3,2,1,0:T(8,128)(2,1)S(1)}, u32[]{:S(2)}, u32[]{:S(2)}) %collective-permute-start.1) | collective-permute-done | bytes 589856 | tf_op jit(solution)/shard_map/ppermute | solution.py:50
  51.1 2.5 collective-permute-start.2
  57.4 13.0 %collective-permute-done.2 = bf16[3,3,256,128]{3,2,1,0:T(8,128)(2,1)S(1)} collective-permute-done((bf16[3,3,256,128]{3,2,1,0:T(8,128)(2,1)S(1)}, bf16[3,3,256,128]{3,2,1,0:T(8,128)(2,1)S(1)}, u32[]{:S(2)}, u32[]{:S(2)}) %collective-permute-start.2) | collective-permute-done | bytes 589856 | tf_op jit(solution)/shard_map/ppermute | solution.py:50
  71.1 2.2 copy-done.3
  73.3 4.9 %fusion.16 = bf16[1,32,32,1024]{3,2,1,0:T(8,128)(2,1)S(1)} fusion(bf16[32,32,3,3,128]{4,1,0,3,2:T(8,128)(2,1)} %bitcast.38, bf16[3,3,2048,128]{3,2,1,0:T(8,128)(2,1)S(1)} %constant_dynamic-update-slice_fusion, s32[]{:T(128)S(6)} %select_n.14), kind=kOutput, calls=%fused_computation.15 | convolution fusion | flops 2416967680 | bytes 6815748 | tf_op jit(solution)/shard_map/bhwpqd,pqcd->bhwc/dot_general | solution.py:34
  78.2 12.2 %copy.60 = bf16[1,32,32,1024]{2,1,0,3:T(8,128)(2,1)} copy(bf16[1,32,32,1024]{3,2,1,0:T(8,128)(2,1)S(1)} %fusion.16) | data formatting | bytes 4194304
  90.3 12.4 %reshape.42 = bf16[1024,1024]{1,0:T(8,128)(2,1)} reshape(bf16[1024,1,32,32]{3,2,1,0:T(8,128)(2,1)} %bitcast.220) | data formatting | bytes 4194304
  102.9 5.2 %fusion.10 = f32[1,32,32,3,3,128]{5,2,4,3,1,0:T(8,128)S(1)} fusion(bf16[3,3,1024,128]{3,2,1,0:T(8,128)(2,1)} %all-gather.6.cloned.1.call-done, bf16[1,32,32,1024]{3,2,1,0:T(8,128)(2,1)} %all-gather.4.cloned.1.call-done), kind=kOutput, calls=%fused_computation.13 | convolution fusion | flops 2415919104 | bytes 9175040 | tf_op jit(solution)/shard_map/bhwc,pqcd->bhwpqd/dot_general | solution.py:14
  108.0 2.1 copy-done.1
  110.2 1.8 slice_bitcast_fusion.17
  111.9 27.3 %reduce-scatter.10.cloned.1.call-done = bf16[128,1024]{1,0:T(8,128)(2,1)} async-done(((bf16[1024,1024]{1,0:T(8,128)(2,1)}), bf16[128,1024]{1,0:T(8,128)(2,1)}) %reduce-scatter.10.cloned.1.call-update) | async-done | bytes 262160
  139.2 1.8 reshape.43
  141.1 1.8 copy.61
  142.9 2.3 multiply_convert_fusion
  147.0 0.9 copy-done.4
  147.8 4.0 %fusion = bf16[3,3,1024,128]{2,3,1,0:T(8,128)(2,1)} fusion(bf16[32,32,3,3,128]{4,1,0,3,2:T(8,128)(2,1)S(1)} %bitcast.223, bf16[1,32,32,1024]{3,2,1,0:T(8,128)(2,1)S(1)} %copy-done.4), kind=kOutput, calls=%fused_computation.3 | convolution fusion | flops 2417098752 | bytes 6815744 | tf_op jit(solution)/shard_map/bhwc,bhwpqd->pqcd/dot_general | solution.py:39
  151.9 23.9 %all-gather.8.cloned.1.call-done = bf16[1,32,32,1024]{3,2,1,0:T(8,128)(2,1)} async-done(((bf16[1,32,32,128]{3,2,1,0:T(8,128)(2,1)}), bf16[1,32,32,1024]{3,2,1,0:T(8,128)(2,1)}) %all-gather.8.cloned.1.call-update) | async-done | bytes 2097168 | tf_op jit(solution)/shard_map/all_gather | solution.py:47
  175.8 4.9 %fusion.4 = bf16[3,3,128,1024,1]{3,2,0,1,4:T(8,128)(2,1)S(1)} fusion(bf16[32,32,3,3,128]{4,1,0,3,2:T(8,128)(2,1)} %bitcast.38, bf16[1,32,32,1024]{3,2,1,0:T(8,128)(2,1)} %all-gather.8.cloned.1.call-done), kind=kOutput, calls=%fused_computation.7 | convolution fusion | flops 2415919104 | bytes 6815744 | tf_op jit(solution)/shard_map/bhwc,bhwpqd->pqcd/dot_general | solution.py:39
  180.7 1.7 copy.83
  182.4 1.6 copy-done.5
  184.0 4.6 %fusion.13 = f32[1,32,32,3,3,128]{5,2,4,3,1,0:T(8,128)S(1)} fusion(bf16[1,32,32,1024]{3,2,1,0:T(8,128)(2,1)S(1)} %copy-done.5, bf16[3,3,2048,128]{3,2,1,0:T(8,128)(2,1)} %copy-done.3, s32[]{:T(128)S(6)} %select_n.14), kind=kOutput, calls=%fused_computation.14 | convolution fusion | flops 2415919104 | bytes 9175044 | tf_op jit(solution)/shard_map/bhwc,pqcd->bhwpqd/dot_general | solution.py:14
  189.3 1.3 fusion.41
  190.6 24.6 %reduce-scatter.6.cloned.1.call-done = bf16[3,3,256,128]{2,3,1,0:T(8,128)(2,1)} async-done(((bf16[3,3,1024,128]{2,3,1,0:T(8,128)(2,1)}), bf16[3,3,256,128]{2,3,1,0:T(8,128)(2,1)}) %reduce-scatter.6.cloned.1.call-update) | async-done | bytes 589840 | tf_op jit(solution)/shard_map/reduce_scatter | solution.py:67
  215.1 2.3 copy.45
  217.5 38.0 %reduce-scatter.8.cloned.1.call-done = bf16[3,3,256,128]{2,3,1,0:T(8,128)(2,1)} async-done(((bf16[3,3,1024,128]{2,3,1,0:T(8,128)(2,1)}), bf16[3,3,256,128]{2,3,1,0:T(8,128)(2,1)}) %reduce-scatter.8.cloned.1.call-update) | async-done | bytes 589840 | tf_op jit(solution)/shard_map/reduce_scatter | solution.py:55
  255.5 2.3 copy.46
  (47 shorter events, 9.3 us)
Async XLA Ops:
  7.2 30.0 %copy-start = (bf16[1,32,32,128]{3,2,1,0:T(8,128)(2,1)S(1)}, bf16[1,32,32,128]{3,2,1,0:T(8,128)(2,1)}, u32[]{:S(2)}) copy-start(bf16[1,32,32,128]{3,2,1,0:T(8,128)(2,1)} %param.7) | copy-start | bytes 786436
  7.2 95.7 %all-gather.6.cloned.1.call-start = ((), (), s32[]{:S(2)}) async-start(), calls=%async_computation.4 | async-start | bytes 2949120 | tf_op jit(solution)/shard_map/all_gather | solution.py:43
  7.9 94.9 %all-gather.4.cloned.1.call-start = ((), (), s32[]{:S(2)}) async-start(), calls=%async_computation.3 | async-start | bytes 2359296 | tf_op jit(solution)/shard_map/all_gather | solution.py:44
  8.7 130.6 %reduce-scatter.10.cloned.1.call-start = ((), (), s32[]{:S(2)}) async-start(), calls=%async_computation.8 | async-start | bytes 2359296
  8.7 21.0 %collective-permute-start = (bf16[3,3,256,128]{3,2,1,0:T(8,128)(2,1)}, bf16[3,3,256,128]{3,2,1,0:T(8,128)(2,1)S(1)}, u32[]{:S(2)}, u32[]{:S(2)}) collective-permute-start(bf16[3,3,256,128]{3,2,1,0:T(8,128)(2,1)} %param.6), channel_id=1, source_target_pairs={{0,8},{8,16},{16,24},{24,0},{1,9},{9,17},{17,25},{25,1},{2,10},{10... | collective-permute-start | bytes 1769480 | tf_op jit(solution)/shard_map/ppermute | solution.py:50
  29.7 21.5 %collective-permute-start.1 = (bf16[3,3,256,128]{3,2,1,0:T(8,128)(2,1)S(1)}, bf16[3,3,256,128]{3,2,1,0:T(8,128)(2,1)S(1)}, u32[]{:S(2)}, u32[]{:S(2)}) collective-permute-start(bf16[3,3,256,128]{3,2,1,0:T(8,128)(2,1)S(1)} %collective-permute-done), channel_id=1, source_target_pairs={{0,8},{8,16},{16,24},{24,0},{1,9},{9,17},{17,25},{25,1},{2,10},{10... | collective-permute-start | bytes 1769480 | tf_op jit(solution)/shard_map/ppermute | solution.py:50
  51.1 19.3 %collective-permute-start.2 = (bf16[3,3,256,128]{3,2,1,0:T(8,128)(2,1)S(1)}, bf16[3,3,256,128]{3,2,1,0:T(8,128)(2,1)S(1)}, u32[]{:S(2)}, u32[]{:S(2)}) collective-permute-start(bf16[3,3,256,128]{3,2,1,0:T(8,128)(2,1)S(1)} %collective-permute-done.1), channel_id=1, source_target_pairs={{0,8},{8,16},{16,24},{24,0},{1,9},{9,17},{17,25},{25,1},{2,10},{10... | collective-permute-start | bytes 1769480 | tf_op jit(solution)/shard_map/ppermute | solution.py:50
  55.9 14.8 %copy-start.2 = (bf16[3,3,256,128]{3,2,1,0:T(8,128)(2,1)S(1)}, bf16[3,3,256,128]{3,2,1,0:T(8,128)(2,1)}, u32[]{:S(2)}) copy-start(bf16[3,3,256,128]{3,2,1,0:T(8,128)(2,1)} %param.6) | copy-start | bytes 1769476
  71.1 2.2 copy-start.3
  102.8 73.0 %all-gather.8.cloned.1.call-start = ((), (), s32[]{:S(2)}) async-start(), calls=%async_computation.5 | async-start | bytes 2359296 | tf_op jit(solution)/shard_map/all_gather | solution.py:47
  108.0 2.1 copy-start.1
  146.0 69.1 %reduce-scatter.6.cloned.1.call-start = ((), (), s32[]{:S(2)}) async-start(), calls=%async_computation.6 | async-start | bytes 2949120 | tf_op jit(solution)/shard_map/reduce_scatter | solution.py:67
  146.2 1.6 copy-start.4
  151.8 103.6 %reduce-scatter.8.cloned.1.call-start = ((), (), s32[]{:S(2)}) async-start(), calls=%async_computation.7 | async-start | bytes 2949120 | tf_op jit(solution)/shard_map/reduce_scatter | solution.py:55
  182.4 1.6 copy-start.5
Sparse Core Ops, SparseCore 0:
  9.9 55.4 all-gather.5
  66.9 30.6 all-gather.3
  102.9 36.3 reduce-scatter.9
  146.1 29.5 all-gather.7
  178.7 36.4 reduce-scatter.5
  218.0 37.3 reduce-scatter.7
